TPU v7x, 128 devices: a whole 4x4x4 slice. The times are simulated.
128 devices in a mesh: req: 16 (over y, x), head: 8 (over z, core).
Axes of the slice: x: 4, y: 4, z: 4, core: 2. Of those that a mesh axis runs over, the one named last changes fastest.
Arguments:
- hidden_in: bfloat16 [8192, 2048], P(('req', 'head')), may hold values from -6 to 6
- segment_ids: int32 [16, 512], P('req', 'head'), may hold values from 0 to 3, never falling along the last dimension, each value on 1 to 256 neighbouring positions
- attn_routes: int32 [8192, 2], P(('req', 'head')), may hold values from 0 to 7, all different within a row; in each aligned block of 512 rows (0 to 511, 512 to 1023, ...) at most 192 rows name the same one
- ffn_routes: int32 [8192, 2], P(('req', 'head')), may hold values from 0 to 7, all different within a row; in each aligned block of 64 rows (0 to 63, 64 to 127, ...) at most 24 rows name the same one
- attn_gain: float32 [2048], replicated, may hold values from 0.1 to 1.9
- attn_router: float32 [2048, 8], replicated, may hold values from -0.125 to 0.125
- w_query: bfloat16 [8, 2048, 2048], P(None, None, 'head'), may hold values from -1 to 1
- w_key: bfloat16 [2048, 2048], P(None, 'head'), may hold values from -32 to 32
- w_value: bfloat16 [2048, 2048], P(None, 'head'), may hold values from -0.125 to 0.125
- w_out: bfloat16 [8, 2048, 2048], P(None, 'head'), may hold values from -0.125 to 0.125
- ffn_gain: float32 [2048], replicated, may hold values from 0.1 to 1.9
- ffn_router: float32 [2048, 8], replicated, may hold values from -0.125 to 0.125
- w_gate_up: bfloat16 [8, 2048, 2, 5632], P('head', None, None, 'req'), may hold values from -0.125 to 0.125
- w_down: bfloat16 [8, 5632, 2048], P('head', 'req'), may hold values from -0.078125 to 0.078125
Outputs:
- layer_out: bfloat16 [8192, 2048], P(('req', 'head'))
Inputs may be any that keep to these rules, and one draw needn't show every extreme that they name: `segment_ids`: within each row segment numbers never fall; each segment has 1 to 256 tokens. `attn_routes`: each token names two different experts; in each aligned block of 512 rows no expert is named by more than 192 rows. `ffn_routes`: each token names two different experts; in each aligned block of 64 rows (the rows of one device) no expert is named by more than 24 rows.
All inputs are finite; a program needn't handle non-finite values.
Results may differ from a plain program's by a relative error of at most 0.015.
Values may be sent and summed in bfloat16 or wider, within the bound.
No kernel may reach another device: no remote copies, remote signals or barrier semaphores. Data moves between devices by JAX's collectives and lax.ppermute only.
A program may use at most 128 MiB of HBM per device.

v0:
```python
import jax
import jax.numpy as jnp
from jax import lax
from jax.sharding import PartitionSpec as P

D = 2048
HD = 128
E_ATT = 8
E_FF = 8
EPSILON = 1e-06
ROPE_BASE = 10000.0


def rms_norm(values, gain_vector):
    widened = values.astype(jnp.float32)
    inverse_rms = lax.rsqrt(jnp.mean(widened * widened, axis=-1, keepdims=True) + EPSILON)
    return (widened * inverse_rms * gain_vector).astype(jnp.bfloat16)


def pair_gates(normed, router, routes):
    logits = jnp.dot(normed.astype(jnp.float32), router, precision=lax.Precision.HIGHEST)
    picked = jnp.take_along_axis(logits, routes, axis=1)
    first_weight = jax.nn.sigmoid(picked[:, 0] - picked[:, 1])
    second_weight = jax.nn.sigmoid(picked[:, 1] - picked[:, 0])
    return jnp.stack([first_weight, second_weight], axis=1)


def positions(segment_row):
    earlier = (segment_row[None, :] < segment_row[:, None]).astype(jnp.int32)
    return jnp.arange(segment_row.shape[0], dtype=jnp.int32) - jnp.sum(earlier, axis=1)


def rotary(values, token_place):
    half_width = values.shape[-1] // 2
    inverse = ROPE_BASE ** (-jnp.arange(half_width, dtype=jnp.float32) / half_width)
    shaped = token_place.astype(jnp.float32).reshape((-1,) + (1,) * (values.ndim - 2) + (1,))
    angles = shaped * inverse
    cosine = jnp.cos(angles)
    sines = jnp.sin(angles)
    lower_half = values[..., :half_width]
    upper_half = values[..., half_width:]
    return jnp.concatenate(
        [lower_half * cosine - upper_half * sines, upper_half * cosine + lower_half * sines],
        axis=-1,
    )


def slot_ranks(experts_flat, expert_count):
    onehot = (experts_flat[:, None] == jnp.arange(expert_count, dtype=jnp.int32)[None, :]).astype(
        jnp.int32
    )
    running = jnp.cumsum(onehot, axis=0) - onehot
    return jnp.sum(running * onehot, axis=1)


def soft_weights(scores, allowed):
    masked = jnp.where(allowed, scores, -1e30)
    largest = jnp.max(masked, axis=-1, keepdims=True)
    exponent = jnp.exp(masked - largest)
    return (exponent / jnp.sum(exponent, axis=-1, keepdims=True)).astype(jnp.bfloat16)


def per_device(
    hidden_in,
    segment_ids,
    attn_routes,
    ffn_routes,
    attn_gain,
    attn_router,
    w_query,
    w_key,
    w_value,
    w_out,
    ffn_gain,
    ffn_router,
    w_gate_up,
    w_down,
):
    row_count = hidden_in.shape[0]
    head_count = lax.axis_size("head")
    seq_length = row_count * head_count
    capacity = 3 * seq_length // 8
    local_width = w_key.shape[1]
    local_heads = local_width // HD
    normed = rms_norm(hidden_in, attn_gain)
    normed_all, segment_all, routes_all = (
        lax.all_gather(normed, "head", axis=0, tiled=True),
        lax.all_gather(segment_ids, "head", axis=1, tiled=True),
        lax.all_gather(attn_routes, "head", axis=0, tiled=True),
    )
    segment_row = segment_all[0]
    token_place = positions(segment_row)
    pair_weights = pair_gates(normed_all, attn_router, routes_all)
    flat_experts = routes_all.reshape(-1)
    slot_index = flat_experts * capacity + slot_ranks(flat_experts, E_ATT)
    slot_table = (
        jnp.full((E_ATT * capacity,), 2 * seq_length, jnp.int32)
        .at[slot_index]
        .set(jnp.arange(2 * seq_length, dtype=jnp.int32))
    )
    padded = jnp.concatenate([normed_all, jnp.zeros((1, D), jnp.bfloat16)], axis=0)
    buffer = padded[slot_table // 2].reshape(E_ATT, capacity, D)
    query_buf = jnp.einsum("ecd,edf->ecf", buffer, w_query, preferred_element_type=jnp.float32)
    queries = query_buf.reshape(E_ATT * capacity, local_width)[slot_index].reshape(
        seq_length, 2, local_heads, HD
    )
    queries = rotary(queries, token_place).astype(jnp.bfloat16)
    key_heads = jnp.dot(normed_all, w_key, preferred_element_type=jnp.float32).reshape(
        seq_length, local_heads, HD
    )
    key_heads = rotary(key_heads, token_place).astype(jnp.bfloat16)
    value_heads = (
        jnp.dot(normed_all, w_value, preferred_element_type=jnp.float32)
        .astype(jnp.bfloat16)
        .reshape(seq_length, local_heads, HD)
    )
    block_rows = min(seq_length, 512)
    block_total = seq_length // block_rows
    key_index = jnp.arange(seq_length, dtype=jnp.int32)

    def attend(block_input):
        query_block, offset = block_input
        scores = jnp.einsum(
            "tjgd,sgd->gjts", query_block, key_heads, preferred_element_type=jnp.float32
        ) * HD ** (-0.5)
        query_index = offset + jnp.arange(block_rows, dtype=jnp.int32)
        allowed = (segment_row[:, None] == segment_row[None, :]) & (
            key_index[None, :] <= query_index[:, None]
        )
        probs = soft_weights(scores, allowed)
        return jnp.einsum(
            "gjts,sgd->tjgd", probs, value_heads, preferred_element_type=jnp.float32
        ).astype(jnp.bfloat16)

    contexts = lax.map(
        attend,
        (
            queries.reshape(block_total, block_rows, 2, local_heads, HD),
            jnp.arange(block_total, dtype=jnp.int32) * block_rows,
        ),
    )
    context = contexts.reshape(2 * seq_length, local_width)
    padded_ctx = jnp.concatenate([context, jnp.zeros((1, local_width), jnp.bfloat16)], axis=0)
    out_buf = padded_ctx[slot_table].reshape(E_ATT, capacity, local_width)
    projected = jnp.einsum("ecf,efd->ecd", out_buf, w_out, preferred_element_type=jnp.float32)
    per_pair = (
        projected.reshape(E_ATT * capacity, D)[slot_index] * pair_weights.reshape(-1)[:, None]
    )
    partial_value = jnp.sum(per_pair.reshape(seq_length, 2, D), axis=1)
    attn_rows = lax.psum_scatter(
        partial_value.astype(jnp.bfloat16), "head", scatter_dimension=0, tiled=True
    ).astype(jnp.float32)
    residual = (hidden_in.astype(jnp.float32) + attn_rows).astype(jnp.bfloat16)
    ffn_normed = rms_norm(residual, ffn_gain)
    ffn_weights = pair_gates(ffn_normed, ffn_router, ffn_routes)
    cap_ffn = 3 * row_count // 8
    local_experts = w_gate_up.shape[0]
    experts_flat = ffn_routes.reshape(-1)
    destination = experts_flat * cap_ffn + slot_ranks(experts_flat, E_FF)
    send_table = (
        jnp.full((E_FF * cap_ffn,), 2 * row_count, jnp.int32)
        .at[destination]
        .set(jnp.arange(2 * row_count, dtype=jnp.int32))
    )
    padded_ffn = jnp.concatenate([ffn_normed, jnp.zeros((1, D), jnp.bfloat16)], axis=0)
    outgoing = padded_ffn[send_table // 2].reshape(head_count, local_experts * cap_ffn, D)
    arrived = lax.all_to_all(outgoing, "head", split_axis=0, concat_axis=0, tiled=True)
    shard_rows = lax.all_gather(arrived, "req", axis=0, tiled=True)
    row_total = shard_rows.shape[0]
    grouped = shard_rows.reshape(row_total, local_experts, cap_ffn, D)
    gate_up = jnp.einsum("mecd,edgf->mecgf", grouped, w_gate_up, preferred_element_type=jnp.float32)
    activated = (jax.nn.silu(gate_up[..., 0, :]) * gate_up[..., 1, :]).astype(jnp.bfloat16)
    partials = jnp.einsum(
        "mecf,efd->mecd", activated, w_down, preferred_element_type=jnp.float32
    ).astype(jnp.bfloat16)
    partials = lax.optimization_barrier(partials).astype(jnp.float32)
    summed = lax.psum_scatter(
        partials.reshape(lax.axis_size("req") * head_count, local_experts * cap_ffn, D).astype(
            jnp.bfloat16
        ),
        "req",
        scatter_dimension=0,
        tiled=True,
    )
    returned = lax.all_to_all(summed, "head", split_axis=0, concat_axis=0, tiled=True)
    expert_rows = returned.reshape(-1, D)[destination]
    mixture = jnp.sum(
        expert_rows.astype(jnp.float32).reshape(row_count, 2, D) * ffn_weights[:, :, None], axis=1
    )
    return (residual.astype(jnp.float32) + mixture).astype(jnp.bfloat16)


def solution(mesh):
    return jax.shard_map(
        per_device,
        mesh=mesh,
        in_specs=(
            P(("req", "head"), None),
            P("req", "head"),
            P(("req", "head"), None),
            P(("req", "head"), None),
            P(),
            P(),
            P(None, None, "head"),
            P(None, "head"),
            P(None, "head"),
            P(None, "head", None),
            P(),
            P(),
            P("head", None, None, "req"),
            P("head", "req", None),
        ),
        out_specs=P(("req", "head"), None),
        check_vma=False,
    )
```

profile of v0, /device:TPU:1, one launch (start us, length us, event | category | flops | bytes accessed | tf_op | source)
XLA Modules:
  0.0 546.9 jit_solution(2003070784256341825)
XLA Ops:
  6.5 1.3 fusion.19
  7.8 1.8 fusion.21
  9.7 13.4 %all-gather = s32[8,64,2]{1,2,0:T(2,128)S(1)} all-gather(s32[1,64,2]{1,2,0:T(2,128)} %bitcast.138), channel_id=1, replica_groups=mesh['req'=16,'head'=8] {'head'}, dimensions={0}, use_global_device_ids=true | all-gather | bytes 4608 | tf_op jit(solution)/shard_map/all_gather | solution.py:89
  23.4 2.3 reduce-window.6
  27.3 1.3 dynamic-slice.1
  29.5 4.3 scatter_custom_fusion
  34.6 5.1 all-reduce.3
  39.9 0.9 fusion.18
  40.8 1.0 multiply_cosine_fusion
  41.9 3.2 concatenate.18
  45.1 15.1 %gather_fusion = bf16[1536,2048]{1,0:T(8,128)(2,1)} fusion(bf16[513,2048]{1,0:T(8,128)(2,1)} %concatenate.18, s32[2048]{0:T(1024)S(1)} %pad_clamp_fusion.1), kind=kCustom, calls=%fused_computation | custom fusion | bytes 12589056 | tf_op jit(solution)/shard_map/gather | solution.py:102
  60.1 8.1 %fusion.53 = f32[8,192,256]{2,1,0:T(8,128)} fusion(bf16[8,192,2048]{2,1,0:T(8,128)(2,1)} %bitcast.127, bf16[8,2048,256]{2,1,0:T(8,128)(2,1)} %param.20), kind=kOutput, calls=%fused_computation.131 | convolution fusion | flops 1610612736 | bytes 16252928 | tf_op jit(solution)/shard_map/ecd,edf->ecf/dot_general | solution.py:103
  68.3 6.1 %gather_fusion.1 = f32[1024,256]{1,0:T(8,128)} fusion(f32[1536,256]{1,0:T(8,128)} %bitcast.125, s32[1024]{0:T(1024)S(1)} %broadcast_clamp_fusion), kind=kCustom, calls=%fused_computation.1 | custom fusion | bytes 2101248 | tf_op jit(solution)/shard_map/gather | solution.py:104
  74.3 2.7 reshape.344
  77.1 4.5 fusion.49
  83.1 2.0 copy.132
  85.1 2.0 copy.133
  87.1 1.8 subtract_convert_fusion
  88.9 1.4 subtract_convert_fusion.1
  91.1 2.1 fusion.51
  94.0 1.2 fusion.17
  95.3 1.3 copy.115
  96.7 5.5 %gather_fusion.2 = bf16[1536,256]{1,0:T(8,128)(2,1)} fusion(bf16[1025,256]{1,0:T(8,128)(2,1)S(1)} %concatenate.20, s32[2048]{0:T(1024)S(1)} %pad_clamp_fusion), kind=kCustom, calls=%fused_computation.2 | custom fusion | bytes 1579008 | tf_op jit(solution)/shard_map/gather | solution.py:144
  102.2 10.0 %fusion.54 = f32[8,192,2048]{2,1,0:T(8,128)} fusion(bf16[8,192,256]{2,1,0:T(8,128)(2,1)} %bitcast.128, bf16[8,256,2048]{2,1,0:T(8,128)(2,1)} %param.23), kind=kOutput, calls=%fused_computation.132 | convolution fusion | flops 1610612736 | bytes 21757952 | tf_op jit(solution)/shard_map/ecf,efd->ecd/dot_general | solution.py:145
  112.3 13.6 %gather_fusion.3 = f32[1024,2048]{1,0:T(8,128)} fusion(f32[1536,2048]{1,0:T(8,128)} %bitcast.124, s32[1024]{0:T(1024)S(1)} %broadcast_clamp_fusion), kind=kCustom, calls=%fused_computation.3 | custom fusion | bytes 16781312 | tf_op jit(solution)/shard_map/gather | solution.py:147
  125.9 10.6 %gather.32 = f32[512,2,2048]{2,1,0:T(2,128)} reshape(f32[1024,2048]{1,0:T(8,128)} %gather_fusion.3) | data formatting | bytes 16777216 | tf_op jit(solution)/shard_map/gather | solution.py:147
  136.5 3.3 fusion.55
  139.8 6.5 %gather_fusion.6 = f32[1024]{0:T(1024)S(1)} fusion(f32[512,8]{0,1:T(8,128)S(1)} %fusion.55, s32[1024]{0:T(1024)S(1)} %reshape.403), kind=kCustom, calls=%fused_computation.6 | custom fusion | bytes 16384 | tf_op jit(solution)/shard_map/jit(take_along_axis)/gather | solution.py:22
  146.9 15.1 %multiply_reduce_fusion = bf16[512,2048]{1,0:T(8,128)(2,1)} fusion(f32[512,2,2048]{2,1,0:T(2,128)} %gather.32, f32[512,2]{1,0:T(8,128)S(1)} %copy.118), kind=kLoop, calls=%fused_computation.14 | loop fusion | flops 3145728 | bytes 10489856 | tf_op jit(solution)/shard_map/reduce_sum | solution.py:149
  163.0 1.0 scatter_custom_fusion.1
  164.1 31.6 %reduce-scatter.3.cloned.1.call-done = bf16[64,2048]{1,0:T(8,128)(2,1)} async-done(((bf16[512,2048]{1,0:T(8,128)(2,1)}), bf16[64,2048]{1,0:T(8,128)(2,1)}) %reduce-scatter.3.cloned.1.call-update) | async-done | bytes 262160 | tf_op jit(solution)/shard_map/reduce_scatter | solution.py:150
  195.7 1.1 fusion.23
  196.8 1.1 fusion.25
  198.6 2.0 gather_fusion.4
  200.7 19.3 %all_to_all.10 = bf16[8,24,2048]{2,1,0:T(8,128)(2,1)S(1)} all-to-all(bf16[8,24,2048]{2,1,0:T(8,128)(2,1)} %bitcast.129), channel_id=1, replica_groups=mesh['req'=16,'head'=8] {'head'}, dimensions={0} | all-to-all | bytes 1572864 | tf_op jit(solution)/shard_map/all_to_all | solution.py:167
  219.9 1.4 copy.121
  221.4 89.2 %all-gather.6.cloned.1.call-done = bf16[128,24,2048]{2,0,1:T(8,128)(2,1)} async-done(((bf16[8,24,2048]{2,0,1:T(8,128)(2,1)}), bf16[128,24,2048]{2,0,1:T(8,128)(2,1)}) %all-gather.6.cloned.1.call-update) | async-done | bytes 12582928 | tf_op jit(solution)/shard_map/all_gather | solution.py:168
  310.6 12.0 %fusion.4 = f32[128,1,24,2,352]{0,4,3,2,1:T(8,128)S(1)} fusion(bf16[128,24,2048]{2,0,1:T(8,128)(2,1)} %all-gather.6.cloned.1.call-done, bf16[1,2048,2,352]{1,3,2,0:T(8,128)(2,1)S(1)} %copy-done), kind=kOutput, calls=%fused_computation.20 | convolution fusion | flops 8858370048 | bytes 24117248 | tf_op jit(solution)/shard_map/mecd,edgf->mecgf/dot_general | solution.py:171
  322.7 9.7 %convert_bitcast_fusion = bf16[128,1,24,2048]{3,0,2,1:T(8,128)(2,1)} fusion(f32[128,1,24,2,352]{0,4,3,2,1:T(8,128)S(1)} %fusion.4, bf16[1,352,2048]{2,1,0:T(8,128)(2,1)S(1)} %copy-done.14), kind=kOutput, calls=%fused_computation.13 | convolution fusion | flops 4441964544 | bytes 22675456 | tf_op jit(solution)/shard_map/mecf,efd->mecd/dot_general | solution.py:173
  334.2 176.1 %all-reduce.7.cloned.1.call-done = bf16[128,24,2048]{2,0,1:T(8,128)(2,1)} async-done(((bf16[128,24,2048]{2,0,1:T(8,128)(2,1)}), bf16[128,24,2048]{2,0,1:T(8,128)(2,1)}) %all-reduce.7.cloned.1.call-update) | async-done | bytes 12582928
  510.3 1.2 constant_dynamic-slice_fusion
  511.5 1.3 copy.122
  512.8 5.3 all-to-all-start.1
  518.4 1.0 gather_fusion.7
  519.8 10.5 %all-to-all-done.1 = bf16[8,24,2048]{2,1,0:T(8,128)(2,1)} async-done(((bf16[8,24,2048]{2,1,0:T(8,128)(2,1)}), bf16[8,24,2048]{2,1,0:T(8,128)(2,1)}, u32[]{:S(2)}, u32[]{:S(2)}) %all-to-all-start.1) | async-done | bytes 786464 | tf_op jit(solution)/shard_map/all_to_all | solution.py:185
  530.3 3.5 gather_fusion.5
  533.8 2.7 reshape.354
  536.5 2.8 multiply_reduce_fusion.1
  (113 shorter events, 11.3 us)
Async XLA Ops:
  6.5 304.1 %copy-start = (bf16[1,2048,2,352]{1,3,2,0:T(8,128)(2,1)S(1)}, bf16[1,2048,2,352]{1,3,2,0:T(8,128)(2,1)}, u32[]{:S(2)}) copy-start(bf16[1,2048,2,352]{1,3,2,0:T(8,128)(2,1)} %param.26) | copy-start | bytes 8650756
  6.5 35.3 %all-gather.4.cloned.1.call-start = ((), (), s32[]{:S(2)}) async-start(), calls=%async_computation.3 | async-start | bytes 2359296 | tf_op jit(solution)/shard_map/all_gather | solution.py:87
  9.6 186.0 %reduce-scatter.3.cloned.1.call-start = ((), (), s32[]{:S(2)}) async-start(), calls=%async_computation.4 | async-start | bytes 2359296 | tf_op jit(solution)/shard_map/reduce_scatter | solution.py:150
  26.4 0.6 copy-start.9
  77.1 4.5 copy-start.1
  77.1 4.5 copy-start.15
  88.9 2.2 copy-start.7
  91.1 2.2 copy-start.2
  91.1 2.2 copy-start.16
  125.9 10.6 %copy-start.8 = (f32[2048,8]{0,1:T(8,128)S(1)}, f32[2048,8]{0,1:T(8,128)}, u32[]{:S(2)}) copy-start(f32[2048,8]{0,1:T(8,128)} %param.19) | copy-start | bytes 196612
  139.8 6.9 %copy-start.10 = (s32[512,2]{0,1:T(2,128)S(1)}, s32[512,2]{0,1:T(2,128)}, u32[]{:S(2)}) copy-start(s32[512,2]{0,1:T(2,128)} %copy-done.9) | copy-start | bytes 12292
  146.9 15.2 %copy-start.12 = (s32[64,2]{0,1:T(2,128)S(1)}, s32[64,2]{0,1:T(2,128)}, u32[]{:S(2)}) copy-start(s32[64,2]{0,1:T(2,128)} %param.17) | copy-start | bytes 1540
  146.9 48.8 %copy-start.3 = (bf16[64,2048]{1,0:T(8,128)(2,1)S(1)}, bf16[64,2048]{1,0:T(8,128)(2,1)}, u32[]{:S(2)}) copy-start(bf16[64,2048]{1,0:T(8,128)(2,1)} %param.14) | copy-start | bytes 786436
  146.9 49.9 %copy-start.13 = (f32[2048]{0:T(1024)S(1)}, f32[2048]{0:T(1024)}, u32[]{:S(2)}) copy-start(f32[2048]{0:T(1024)} %param.24) | copy-start | bytes 24580
  162.0 148.6 %all-gather.6.cloned.1.call-start = ((), (), s32[]{:S(2)}) async-start(), calls=%async_computation.5 | async-start | bytes 13369344 | tf_op jit(solution)/shard_map/all_gather | solution.py:168
  197.9 0.7 copy-start.5
  221.3 288.9 %all-reduce.7.cloned.1.call-start = ((), (), s32[]{:S(2)}) async-start(), calls=%async_computation.6 | async-start | bytes 25165824
  310.6 12.0 %copy-start.14 = (bf16[1,352,2048]{2,1,0:T(8,128)(2,1)S(1)}, bf16[1,352,2048]{2,1,0:T(8,128)(2,1)}, u32[]{:S(2)}) copy-start(bf16[1,352,2048]{2,1,0:T(8,128)(2,1)} %param.27) | copy-start | bytes 4325380
  332.3 0.7 copy-start.17
  332.4 185.7 %copy-start.6 = (bf16[64,2048]{1,0:T(8,128)(2,1)S(1)}, bf16[64,2048]{1,0:T(8,128)(2,1)}, u32[]{:S(2)}) copy-start(bf16[64,2048]{1,0:T(8,128)(2,1)} %copy-done.5) | copy-start | bytes 786436
  332.4 185.7 %copy-start.11 = (f32[2048,8]{0,1:T(8,128)S(1)}, f32[2048,8]{0,1:T(8,128)}, u32[]{:S(2)}) copy-start(f32[2048,8]{0,1:T(8,128)} %param.25) | copy-start | bytes 196612
  512.8 17.5 %all-to-all-start.1 = ((bf16[8,24,2048]{2,1,0:T(8,128)(2,1)}), bf16[8,24,2048]{2,1,0:T(8,128)(2,1)}, u32[]{:S(2)}, u32[]{:S(2)}) async-start(bf16[8,24,2048]{2,1,0:T(8,128)(2,1)} %copy.122), calls=%async_computation.2 | async-start | bytes 1572864 | tf_op jit(solution)/shard_map/all_to_all | solution.py:185
  519.4 19.9 %copy-start.4 = (bf16[64,2048]{1,0:T(8,128)(2,1)S(1)}, bf16[64,2048]{1,0:T(8,128)(2,1)}, u32[]{:S(2)}) copy-start(bf16[64,2048]{1,0:T(8,128)(2,1)} %reduce-scatter.3.cloned.1.call-done) | copy-start | bytes 786436
Sparse Core Ops, SparseCore 0:
  9.7 29.1 all-gather.3
  162.2 33.4 reduce-scatter.2
  221.4 89.1 all-gather.5
  332.5 177.7 all-reduce.6
where the time goes:
time: 552 us; the launch traced here: 547 us
  waiting for transfers between devices  308 us (56%)
  local copies, waits for them, and re-layouts  99.4 us (18%)
  matrix products  47 us (9%)
  blocking collectives  37.8 us (7%)
  other arithmetic  34.5 us (6%)
  between operations  15.2 us (3%)
    unnamed x5, waiting for transfers between devices  176 us
    all_gather x1, waiting for transfers between devices, per_device(): shard_rows = lax.all_gather(arrived, 'req', axis=0, tiled=True)  89.2 us
    reduce_scatter x1, waiting for transfers between devices, per_device(): lax.psum_scatter(partial_value.astype(jnp.bfloat16), 'head', scatter_dime...  31.6 us
    gather x2, local copies, waits for them, and re-layouts, per_device(): projected.reshape(E_ATT * capacity, D)[slot_index]  24.2 us
    all_to_all x1, blocking collectives, per_device(): lax.all_to_all(outgoing, 'head', split_axis=0, concat_axis=0, tiled=True)  19.3 us
    reduce_sum x1, other arithmetic, per_device(): partial_value = jnp.sum(per_pair.reshape(seq_length, 2, D), axis=1)  15.1 us
    gather x1, local copies, waits for them, and re-layouts, per_device(): buffer = padded[slot_table // 2].reshape(E_ATT, capacity, D)  15.1 us
    all_gather x1, blocking collectives, per_device(): lax.all_gather(attn_routes, 'head', axis=0, tiled=True)  13.4 us
  transfers between devices with their start and end apart: 5, of which 4 were waited for; matrix products, arithmetic and copies ran while one was open for 3% of the time, Pallas kernels for 0%

commit v1 on v0

--- a/solution.py
+++ b/solution.py
@@ -165,7 +165,9 @@
     padded_ffn = jnp.concatenate([ffn_normed, jnp.zeros((1, D), jnp.bfloat16)], axis=0)
     outgoing = padded_ffn[send_table // 2].reshape(head_count, local_experts * cap_ffn, D)
     arrived = lax.all_to_all(outgoing, "head", split_axis=0, concat_axis=0, tiled=True)
-    shard_rows = lax.all_gather(arrived, "req", axis=0, tiled=True)
+    shard_rows = jnp.concatenate(
+        lax.all_to_all(jnp.stack([arrived] * lax.axis_size("req")), "req", 0, 0), axis=0
+    )
     row_total = shard_rows.shape[0]
     grouped = shard_rows.reshape(row_total, local_experts, cap_ffn, D)
     gate_up = jnp.einsum("mecd,edgf->mecgf", grouped, w_gate_up, preferred_element_type=jnp.float32)

time: 552 us -> 613 us (1.11)
  blocking collectives: 37.8 us -> 184 us
  waiting for transfers between devices: 308 us -> 215 us
  local copies, waits for them, and re-layouts: 99.4 us -> 107 us
    all_to_all x0 -> x1, blocking collectives: none -> 146 us  [per_device(): lax.all_to_all(jnp.stack([arrived] * lax.axis_size('req')), 'req', 0, 0)]
    all_gather x1 -> x0, waiting for transfers between devices: 89.2 us -> none  [per_device(): shard_rows = lax.all_gather(arrived, 'req', axis=0, tiled=True)]
    another operation x0 -> x1, local copies, waits for them, and re-layouts: none -> 7.31 us  [per_device(): jnp.stack([arrived] * lax.axis_size('req'))]
    unnamed x5 -> x4, waiting for transfers between devices: 176 us -> 173 us
  transfers between devices with their start and end apart: 5 -> 4, of which waited for: 4 -> 3; matrix products, arithmetic and copies ran while one was open for 3% -> 3% of each run, Pallas kernels for 0% -> 0%
where the time goes in v1:
time: 613 us; the launch traced here: 608 us
  waiting for transfers between devices  215 us (35%)
  blocking collectives  184 us (30%)
  local copies, waits for them, and re-layouts  107 us (17%)
  matrix products  46 us (8%)
  other arithmetic  34.5 us (6%)
  between operations  15.3 us (2%)
    unnamed x4, waiting for transfers between devices  173 us
    all_to_all x1, blocking collectives, per_device(): lax.all_to_all(jnp.stack([arrived] * lax.axis_size('req')), 'req', 0, 0)  146 us
    reduce_scatter x1, waiting for transfers between devices, per_device(): lax.psum_scatter(partial_value.astype(jnp.bfloat16), 'head', scatter_dime...  31.6 us
    gather x2, local copies, waits for them, and re-layouts, per_device(): projected.reshape(E_ATT * capacity, D)[slot_index]  24.2 us
    all_to_all x1, blocking collectives, per_device(): lax.all_to_all(outgoing, 'head', split_axis=0, concat_axis=0, tiled=True)  19.3 us
    gather x1, local copies, waits for them, and re-layouts, per_device(): buffer = padded[slot_table // 2].reshape(E_ATT, capacity, D)  15.1 us
    reduce_sum x1, other arithmetic, per_device(): partial_value = jnp.sum(per_pair.reshape(seq_length, 2, D), axis=1)  15.1 us
    all_gather x1, blocking collectives, per_device(): lax.all_gather(attn_routes, 'head', axis=0, tiled=True)  13.4 us
  transfers between devices with their start and end apart: 4, of which 3 were waited for; matrix products, arithmetic and copies ran while one was open for 3% of the time, Pallas kernels for 0%

profile of v1, /device:TPU:1, one launch (start us, length us, event | category | flops | bytes accessed | tf_op | source)
XLA Modules:
  0.0 607.6 jit_solution(16110153669978228963)
XLA Ops:
  6.5 1.3 fusion.20
  7.8 1.8 fusion.22
  9.7 13.4 %all-gather = s32[8,64,2]{1,2,0:T(2,128)S(1)} all-gather(s32[1,64,2]{1,2,0:T(2,128)} %bitcast.140), channel_id=1, replica_groups=mesh['req'=16,'head'=8] {'head'}, dimensions={0}, use_global_device_ids=true | all-gather | bytes 4608 | tf_op jit(solution)/shard_map/all_gather | solution.py:89
  23.4 2.3 reduce-window.6
  27.3 1.3 dynamic-slice.1
  29.5 4.3 scatter_custom_fusion
  34.6 5.1 all-reduce.3
  40.8 1.0 multiply_cosine_fusion
  41.9 3.2 concatenate.18
  45.1 15.1 %gather_fusion = bf16[1536,2048]{1,0:T(8,128)(2,1)} fusion(bf16[513,2048]{1,0:T(8,128)(2,1)} %concatenate.18, s32[2048]{0:T(1024)S(1)} %pad_clamp_fusion.1), kind=kCustom, calls=%fused_computation | custom fusion | bytes 12589056 | tf_op jit(solution)/shard_map/gather | solution.py:102
  60.2 8.1 %fusion.54 = f32[8,192,256]{2,1,0:T(8,128)} fusion(bf16[8,192,2048]{2,1,0:T(8,128)(2,1)} %bitcast.129, bf16[8,2048,256]{2,1,0:T(8,128)(2,1)} %param.20), kind=kOutput, calls=%fused_computation.132 | convolution fusion | flops 1610612736 | bytes 16252928 | tf_op jit(solution)/shard_map/ecd,edf->ecf/dot_general | solution.py:103
  68.3 6.1 gather_fusion.1
  74.4 2.7 reshape.347
  77.1 4.3 fusion.50
  81.5 2.6 fusion.53
  84.9 2.0 copy.136
  86.9 2.0 copy.137
  88.8 1.8 subtract_convert_fusion
  90.7 1.4 subtract_convert_fusion.1
  92.9 2.1 fusion.52
  95.8 1.2 fusion.18
  97.0 1.3 copy.118
  98.5 5.5 gather_fusion.2
  104.0 10.0 %fusion.55 = f32[8,192,2048]{2,1,0:T(8,128)} fusion(bf16[8,192,256]{2,1,0:T(8,128)(2,1)} %bitcast.130, bf16[8,256,2048]{2,1,0:T(8,128)(2,1)} %param.23), kind=kOutput, calls=%fused_computation.133 | convolution fusion | flops 1610612736 | bytes 21757952 | tf_op jit(solution)/shard_map/ecf,efd->ecd/dot_general | solution.py:145
  114.0 13.6 %gather_fusion.3 = f32[1024,2048]{1,0:T(8,128)} fusion(f32[1536,2048]{1,0:T(8,128)} %bitcast.126, s32[1024]{0:T(1024)S(1)} %broadcast_clamp_fusion), kind=kCustom, calls=%fused_computation.3 | custom fusion | bytes 16781312 | tf_op jit(solution)/shard_map/gather | solution.py:147
  127.7 10.6 %gather.32 = f32[512,2,2048]{2,1,0:T(2,128)} reshape(f32[1024,2048]{1,0:T(8,128)} %gather_fusion.3) | data formatting | bytes 16777216 | tf_op jit(solution)/shard_map/gather | solution.py:147
  138.3 3.3 fusion.56
  141.6 6.5 %gather_fusion.6 = f32[1024]{0:T(1024)S(1)} fusion(f32[512,8]{0,1:T(8,128)S(1)} %fusion.56, s32[1024]{0:T(1024)S(1)} %reshape.407), kind=kCustom, calls=%fused_computation.6 | custom fusion | bytes 16384 | tf_op jit(solution)/shard_map/jit(take_along_axis)/gather | solution.py:22
  148.7 15.1 %multiply_reduce_fusion = bf16[512,2048]{1,0:T(8,128)(2,1)} fusion(f32[512,2,2048]{2,1,0:T(2,128)} %gather.32, f32[512,2]{1,0:T(8,128)S(1)} %copy.121), kind=kLoop, calls=%fused_computation.15 | loop fusion | flops 3145728 | bytes 10489856 | tf_op jit(solution)/shard_map/reduce_sum | solution.py:149
  165.8 31.6 %reduce-scatter.3.cloned.1.call-done = bf16[64,2048]{1,0:T(8,128)(2,1)} async-done(((bf16[512,2048]{1,0:T(8,128)(2,1)}), bf16[64,2048]{1,0:T(8,128)(2,1)}) %reduce-scatter.3.cloned.1.call-update) | async-done | bytes 262160 | tf_op jit(solution)/shard_map/reduce_scatter | solution.py:150
  197.4 1.1 fusion.24
  198.6 1.1 fusion.26
  200.4 2.0 gather_fusion.4
  202.4 19.3 %all_to_all.15 = bf16[8,24,2048]{2,1,0:T(8,128)(2,1)S(1)} all-to-all(bf16[8,24,2048]{2,1,0:T(8,128)(2,1)} %bitcast.131), channel_id=1, replica_groups=mesh['req'=16,'head'=8] {'head'}, dimensions={0} | all-to-all | bytes 1572864 | tf_op jit(solution)/shard_map/all_to_all | solution.py:167
  221.7 1.4 copy.124
  223.1 7.3 %stack.7 = bf16[16,8,24,2048]{3,1,2,0:T(8,128)(2,1)} broadcast(bf16[8,24,2048]{2,0,1:T(8,128)(2,1)} %copy.124), dimensions={1,2,3} | broadcast | bytes 13369344 | tf_op jit(solution)/shard_map/stack | solution.py:169
  230.4 146.3 %all_to_all.16 = bf16[16,8,24,2048]{3,1,2,0:T(8,128)(2,1)S(1)} all-to-all(bf16[16,8,24,2048]{3,1,2,0:T(8,128)(2,1)} %stack.7), channel_id=1, replica_groups=mesh['req'=16,'head'=8] {'req'}, dimensions={0} | all-to-all | bytes 25165824 | tf_op jit(solution)/shard_map/all_to_all | solution.py:169
  376.7 9.1 %fusion.5 = f32[128,1,24,2,352]{0,4,3,2,1:T(8,128)S(1)} fusion(bf16[16,8,24,2048]{3,1,2,0:T(8,128)(2,1)S(1)} %all_to_all.16, bf16[1,2048,2,352]{1,3,2,0:T(8,128)(2,1)S(1)} %copy-done), kind=kOutput, calls=%fused_computation.21 | convolution fusion | flops 8858370048 | bytes 24117248 | tf_op jit(solution)/shard_map/mecd,edgf->mecgf/dot_general | solution.py:173
  385.9 9.7 %convert_bitcast_fusion = bf16[128,1,24,2048]{3,0,2,1:T(8,128)(2,1)} fusion(f32[128,1,24,2,352]{0,4,3,2,1:T(8,128)S(1)} %fusion.5, bf16[1,352,2048]{2,1,0:T(8,128)(2,1)S(1)} %copy-done.13), kind=kOutput, calls=%fused_computation.14 | convolution fusion | flops 4441964544 | bytes 22675456 | tf_op jit(solution)/shard_map/mecf,efd->mecd/dot_general | solution.py:175
  397.4 173.3 %all-reduce.7.cloned.1.call-done = bf16[128,24,2048]{2,0,1:T(8,128)(2,1)} async-done(((bf16[128,24,2048]{2,0,1:T(8,128)(2,1)}), bf16[128,24,2048]{2,0,1:T(8,128)(2,1)}) %all-reduce.7.cloned.1.call-update) | async-done | bytes 12582928
  570.7 1.2 constant_dynamic-slice_fusion
  571.9 1.3 copy.126
  573.3 5.6 all-to-all-start.2
  579.2 1.0 gather_fusion.7
  580.6 10.5 %all-to-all-done.2 = bf16[8,24,2048]{2,1,0:T(8,128)(2,1)} async-done(((bf16[8,24,2048]{2,1,0:T(8,128)(2,1)}), bf16[8,24,2048]{2,1,0:T(8,128)(2,1)}, u32[]{:S(2)}, u32[]{:S(2)}) %all-to-all-start.2) | async-done | bytes 786464 | tf_op jit(solution)/shard_map/all_to_all | solution.py:187
  591.0 3.5 gather_fusion.5
  594.5 2.7 reshape.358
  597.2 2.8 multiply_reduce_fusion.1
  (108 shorter events, 12.4 us)
Async XLA Ops:
  6.5 370.2 %copy-start = (bf16[1,2048,2,352]{1,3,2,0:T(8,128)(2,1)S(1)}, bf16[1,2048,2,352]{1,3,2,0:T(8,128)(2,1)}, u32[]{:S(2)}) copy-start(bf16[1,2048,2,352]{1,3,2,0:T(8,128)(2,1)} %param.26) | copy-start | bytes 8650756
  6.5 35.3 %all-gather.3.cloned.1.call-start = ((), (), s32[]{:S(2)}) async-start(), calls=%async_computation.4 | async-start | bytes 2359296 | tf_op jit(solution)/shard_map/all_gather | solution.py:87
  9.6 187.8 %reduce-scatter.3.cloned.1.call-start = ((), (), s32[]{:S(2)}) async-start(), calls=%async_computation.5 | async-start | bytes 2359296 | tf_op jit(solution)/shard_map/reduce_scatter | solution.py:150
  26.4 0.6 copy-start.8
  90.6 2.2 copy-start.6
  92.9 2.2 copy-start.1
  92.9 2.2 copy-start.14
  127.7 10.6 %copy-start.7 = (f32[2048,8]{0,1:T(8,128)S(1)}, f32[2048,8]{0,1:T(8,128)}, u32[]{:S(2)}) copy-start(f32[2048,8]{0,1:T(8,128)} %param.19) | copy-start | bytes 196612
  141.6 6.9 %copy-start.9 = (s32[512,2]{0,1:T(2,128)S(1)}, s32[512,2]{0,1:T(2,128)}, u32[]{:S(2)}) copy-start(s32[512,2]{0,1:T(2,128)} %copy-done.8) | copy-start | bytes 12292
  148.6 15.2 %copy-start.11 = (s32[64,2]{0,1:T(2,128)S(1)}, s32[64,2]{0,1:T(2,128)}, u32[]{:S(2)}) copy-start(s32[64,2]{0,1:T(2,128)} %param.17) | copy-start | bytes 1540
  148.7 48.8 %copy-start.2 = (bf16[64,2048]{1,0:T(8,128)(2,1)S(1)}, bf16[64,2048]{1,0:T(8,128)(2,1)}, u32[]{:S(2)}) copy-start(bf16[64,2048]{1,0:T(8,128)(2,1)} %param.14) | copy-start | bytes 786436
  148.7 49.9 %copy-start.12 = (f32[2048]{0:T(1024)S(1)}, f32[2048]{0:T(1024)}, u32[]{:S(2)}) copy-start(f32[2048]{0:T(1024)} %param.24) | copy-start | bytes 24580
  163.8 406.9 %all-reduce.7.cloned.1.call-start = ((), (), s32[]{:S(2)}) async-start(), calls=%async_computation.6 | async-start | bytes 25165824
  199.7 0.7 copy-start.4
  376.7 9.2 %copy-start.13 = (bf16[1,352,2048]{2,1,0:T(8,128)(2,1)S(1)}, bf16[1,352,2048]{2,1,0:T(8,128)(2,1)}, u32[]{:S(2)}) copy-start(bf16[1,352,2048]{2,1,0:T(8,128)(2,1)} %param.27) | copy-start | bytes 4325380
  395.6 0.7 copy-start.15
  395.6 183.2 %copy-start.5 = (bf16[64,2048]{1,0:T(8,128)(2,1)S(1)}, bf16[64,2048]{1,0:T(8,128)(2,1)}, u32[]{:S(2)}) copy-start(bf16[64,2048]{1,0:T(8,128)(2,1)} %copy-done.4) | copy-start | bytes 786436
  395.6 183.2 %copy-start.10 = (f32[2048,8]{0,1:T(8,128)S(1)}, f32[2048,8]{0,1:T(8,128)}, u32[]{:S(2)}) copy-start(f32[2048,8]{0,1:T(8,128)} %param.25) | copy-start | bytes 196612
  573.3 17.8 %all-to-all-start.2 = ((bf16[8,24,2048]{2,1,0:T(8,128)(2,1)}), bf16[8,24,2048]{2,1,0:T(8,128)(2,1)}, u32[]{:S(2)}, u32[]{:S(2)}) async-start(bf16[8,24,2048]{2,1,0:T(8,128)(2,1)} %copy.126), calls=%async_computation.3 | async-start | bytes 1572864 | tf_op jit(solution)/shard_map/all_to_all | solution.py:187
  580.2 19.8 %copy-start.3 = (bf16[64,2048]{1,0:T(8,128)(2,1)S(1)}, bf16[64,2048]{1,0:T(8,128)(2,1)}, u32[]{:S(2)}) copy-start(bf16[64,2048]{1,0:T(8,128)(2,1)} %reduce-scatter.3.cloned.1.call-done) | copy-start | bytes 786436
Sparse Core Ops, SparseCore 0:
  9.7 29.1 all-gather.2
  163.9 33.4 reduce-scatter.2
  395.7 174.9 all-reduce.6
